TPU v7x, 32 devices: a whole 2x2x4 slice. The times are simulated.
32 devices in a mesh: section: 4 (over x, core), dp: 8 (over z, y).
Axes of the slice: x: 2, y: 2, z: 4, core: 2. Of those that a mesh axis runs over, the one named last changes fastest.
Arguments:
- token_ids: int32 [2, 16], P(None, 'dp'), may hold values from 0 to 8191
- target_ids: int32 [2, 16], P(None, 'dp'), may hold values from 0 to 8191
- table: bfloat16 [8192, 4608], P(('section', 'dp')), may hold values from -0.06629126 to 0.06629126
- norm_gain: bfloat16 [2, 4, 4608], P(None, 'section'), may hold values from 0.099609375 to 1.8984375
- w_in: bfloat16 [2, 4, 8, 4608], P(None, 'section'), may hold values from -0.09375 to 0.09375
- w_out: bfloat16 [2, 4, 8, 4608], P(None, 'section'), may hold values from -2 to 2
- final_gain: bfloat16 [4608], replicated, may hold values from 0.099609375 to 1.8984375
Outputs:
- token_loss: float32 [2, 16], P(None, 'dp')
- table_grad: bfloat16 [8192, 4608], P(('section', 'dp'))
All inputs are finite; a program needn't handle non-finite values.
Results may differ from a plain program's by a relative error of at most 0.013.
The roundings to bfloat16 on the way count: a program that leaves them out, or rounds other values in their place, can miss the bound.
Values may be sent and summed in bfloat16 or wider, within the bound.
A program may use at most 64 MiB of HBM per device.

v0:
```python
import math
import jax
import jax.numpy as jnp
from jax import lax
from jax.sharding import PartitionSpec as P

EPS = 1e-06
CAP = 30.0
GELU_C = 0.7978845608028654


def shifted(block, axis, distance):
    devices = range(lax.axis_size(axis))
    route = [((i - distance) % len(devices), i) for i in devices]
    return lax.ppermute(block, axis, route)


def from_root(block, axis, source):
    block = jnp.where(lax.axis_index(axis) == source, block, jnp.zeros_like(block))
    return lax.psum(block, axis)


def gelu_tanh(values):
    return 0.5 * values * (1.0 + jnp.tanh(GELU_C * (values + 0.044715 * values * values * values)))


def gelu_slope(values):
    inner = jnp.tanh(GELU_C * (values + 0.044715 * values * values * values))
    return 0.5 * (1.0 + inner) + 0.5 * values * (1.0 - inner * inner) * GELU_C * (
        1.0 + 3.0 * 0.044715 * values * values
    )


def normalize(rows_in):
    values = rows_in.astype(jnp.float32)
    scale = lax.rsqrt(jnp.mean(values * values, axis=-1, keepdims=True) + EPS)
    return (values * scale, scale)


def norm_back(normed, scale, grad):
    return scale * (grad - normed * jnp.mean(grad * normed, axis=-1, keepdims=True))


def layer_forward(rows_in, gain, first_proj, second_proj):
    normed, scale = normalize(rows_in)
    activated = (normed * gain.astype(jnp.float32)).astype(jnp.bfloat16)
    preact = lax.dot_general(
        activated, first_proj, (((1,), (1,)), ((), ())), preferred_element_type=jnp.float32
    )
    hidden = gelu_tanh(preact).astype(jnp.bfloat16)
    branch = jnp.dot(hidden, second_proj, preferred_element_type=jnp.float32)
    return (rows_in.astype(jnp.float32) + branch).astype(jnp.bfloat16)


def layer_backward(rows_in, gain, first_proj, second_proj, grad_out):
    normed, scale = normalize(rows_in)
    gain_float = gain.astype(jnp.float32)
    activated = (normed * gain_float).astype(jnp.bfloat16)
    preact = lax.dot_general(
        activated, first_proj, (((1,), (1,)), ((), ())), preferred_element_type=jnp.float32
    )
    hidden_grad = lax.dot_general(
        grad_out, second_proj, (((1,), (1,)), ((), ())), preferred_element_type=jnp.float32
    )
    preact_grad = (hidden_grad * gelu_slope(preact)).astype(jnp.bfloat16)
    act_grad = jnp.dot(preact_grad, first_proj, preferred_element_type=jnp.float32)
    return (grad_out.astype(jnp.float32) + norm_back(normed, scale, act_grad * gain_float)).astype(
        jnp.bfloat16
    )


def per_device(token_ids, target_ids, table, norm_gain, w_in, w_out, final_gain):
    sections = lax.axis_size("section")
    section_index = lax.axis_index("section")
    replicas = lax.axis_size("dp")
    replica_index = lax.axis_index("dp")
    batches, width = token_ids.shape
    rows_dev, dim = table.shape
    embed_scale = math.sqrt(dim)
    offset = (section_index * replicas + replica_index) * rows_dev
    columns = jnp.arange(rows_dev, dtype=jnp.int32)
    final_scale = final_gain.astype(jnp.float32)
    ids = lax.all_gather(jnp.concatenate([token_ids, target_ids], 0), "dp", axis=1, tiled=True)
    gains = lax.all_gather(norm_gain, "section", axis=1, tiled=True).reshape(-1, dim)
    first = lax.all_gather(w_in, "section", axis=1, tiled=True).reshape(2 * sections, -1, dim)
    second = lax.all_gather(w_out, "section", axis=1, tiled=True).reshape(2 * sections, -1, dim)
    all_inputs, all_targets = (ids[:batches], ids[batches:])
    wide = all_inputs.shape[1]
    token_count = batches * wide
    chosen = ((all_inputs.reshape(token_count) - offset)[:, None] == columns[None, :]).astype(
        jnp.bfloat16
    )
    looked = jnp.dot(chosen, table, preferred_element_type=jnp.float32).astype(jnp.bfloat16)
    looked = lax.psum(looked, ("section", "dp")).astype(jnp.float32)
    rows = (looked * embed_scale).astype(jnp.bfloat16)

    def forward(rows, weights):
        return (layer_forward(rows, *weights), rows)

    rows, inputs = lax.scan(forward, rows, (gains, first, second))
    normed, scale = normalize(rows)
    head_input = (normed * final_scale).astype(jnp.bfloat16)
    scores = lax.dot_general(
        head_input, table, (((1,), (1,)), ((), ())), preferred_element_type=jnp.float32
    )
    squash = jnp.tanh(scores / CAP)
    capped = CAP * squash
    powers = jnp.exp(capped)
    goal_local = all_targets.reshape(token_count) - offset
    target_mask = goal_local[:, None] == columns[None, :]
    stats = lax.psum(
        jnp.stack(
            [
                jnp.sum(powers, axis=1),
                jnp.sum(jnp.where(target_mask, capped, jnp.float32(0.0)), axis=1),
            ]
        ),
        ("section", "dp"),
    )
    exp_total, target_score = (stats[0], stats[1])
    loss_all = (jnp.log(exp_total) - target_score).reshape(batches, wide)
    token_loss = lax.dynamic_slice_in_dim(loss_all, replica_index * width, width, 1)
    score_grad = (
        (powers / exp_total[:, None] - target_mask.astype(jnp.float32)) * (1.0 - squash * squash)
    ).astype(jnp.bfloat16)
    partial_value = jnp.dot(score_grad, table, preferred_element_type=jnp.float32)
    head_in_grad = lax.psum(partial_value, ("section", "dp"))
    grad = norm_back(normed, scale, head_in_grad * final_scale).astype(jnp.bfloat16)

    def backward(grad, saved):
        return (layer_backward(*saved, grad), None)

    grad, _ = lax.scan(backward, grad, (inputs, gains, first, second), reverse=True)
    head_grad = lax.dot_general(
        score_grad, head_input, (((0,), (0,)), ((), ())), preferred_element_type=jnp.float32
    )
    embed_grad = (
        lax.dot_general(chosen, grad, (((0,), (0,)), ((), ())), preferred_element_type=jnp.float32)
        * embed_scale
    )
    return (token_loss, (head_grad + embed_grad).astype(jnp.bfloat16))


def solution(mesh):
    return jax.shard_map(
        per_device,
        mesh=mesh,
        in_specs=(
            P(None, "dp"),
            P(None, "dp"),
            P(("section", "dp"), None),
            P(None, "section", None),
            P(None, "section", None, None),
            P(None, "section", None, None),
            P(),
        ),
        out_specs=(P(None, "dp"), P(("section", "dp"), None)),
        check_vma=False,
    )
```

profile of v0, /device:TPU:0, one launch (start us, length us, event | category | flops | bytes accessed | tf_op | source)
XLA Modules:
  0.0 419.9 jit_solution(2897440791546498494)
XLA Ops:
  8.2 22.3 %all-gather = s32[8,2,4]{2,1,0:T(2,128)S(1)} all-gather(s32[1,2,4]{2,1,0:T(2,128)S(1)} %bitcast.102), channel_id=1, replica_groups=mesh['section'=4,'dp'=8] {'dp'}, dimensions={0}, use_global_device_ids=true | all-gather | bytes 288 | tf_op jit(solution)/shard_map/all_gather | solution.py:83
  30.6 1.2 convolution_convert_fusion
  32.1 5.3 %all_gather.13 = bf16[2,4,4608]{2,0,1:T(2,128)(2,1)S(1)} all-gather(bf16[2,1,4608]{2,0,1:T(2,128)(2,1)S(1)} %copy-done.3), channel_id=1, replica_groups=mesh['section'=4,'dp'=8] {'section'}, dimensions={1}, use_global_device_ids=true | all-gather | bytes 92160 | tf_op jit(solution)/shard_map/all_gather | solution.py:84
  38.0 8.2 %all_gather.14 = bf16[2,4,8,4608]{3,2,1,0:T(8,128)(2,1)} all-gather(bf16[2,1,8,4608]{3,2,1,0:T(8,128)(2,1)S(1)} %copy-done.1), channel_id=1, replica_groups=mesh['section'=4,'dp'=8] {'section'}, dimensions={1}, use_global_device_ids=true | all-gather | bytes 737280 | tf_op jit(solution)/shard_map/all_gather | solution.py:85
  46.2 8.1 %all_gather.15 = bf16[2,4,8,4608]{3,2,1,0:T(8,128)(2,1)} all-gather(bf16[2,1,8,4608]{3,2,1,0:T(8,128)(2,1)S(1)} %copy-done.2), channel_id=1, replica_groups=mesh['section'=4,'dp'=8] {'section'}, dimensions={1}, use_global_device_ids=true | all-gather | bytes 737280 | tf_op jit(solution)/shard_map/all_gather | solution.py:86
  54.3 100.7 %all-reduce.3.cloned.1.call-done = bf16[32,4608]{1,0:T(8,128)(2,1)} async-done(((bf16[32,4608]{1,0:T(8,128)(2,1)}), bf16[32,4608]{1,0:T(8,128)(2,1)}) %all-reduce.3.cloned.1.call-update) | async-done | bytes 294928 | tf_op jit(solution)/shard_map/psum | solution.py:94
  156.0 28.2 %while.26 = (s32[]{:T(128)}, bf16[32,4608]{1,0:T(8,128)(2,1)S(1)}, bf16[8,32,4608]{2,1,0:T(8,128)(2,1)}, bf16[8,4608]{1,0:T(8,128)(2,1)}, bf16[8,8,4608]{2,1,0:T...) while((s32[]{:T(128)}, bf16[32,4608]{1,0:T(8,128)(2,1)S(1)}, bf16[8,32,4608]{2,1,0:T(8,128)(2,1)}, ...), condition=%wide.region_3.4_spmd, body=%wide.region_1.3_spmd.sunk | while | flops 6200098 | bytes 2556893 | solution.py:100
  157.9 1.6 fusion.132
  161.5 1.6 fusion.132
  165.0 1.6 fusion.132
  168.5 1.6 fusion.132
  172.1 1.6 fusion.132
  175.6 1.6 fusion.132
  179.1 1.6 fusion.132
  182.7 1.6 fusion.132
  185.4 41.2 %psum.22 = f32[2,32]{1,0:T(2,128)S(1)} all-reduce(f32[2,32]{1,0:T(2,128)S(1)} %pad_maximum_fusion), channel_id=1, replica_groups=mesh['section'=4,'dp'=8] {'section','dp'}, use_global_device_ids=true, to_apply=%region_7.8 | all-reduce | flops 64 | bytes 512 | tf_op jit(solution)/shard_map/psum | solution.py:111
  226.7 1.4 fusion.107
  228.8 3.0 fusion.102
  231.8 123.7 %all-reduce.5.cloned.1.call-done = f32[32,4608]{1,0:T(8,128)} async-done(((f32[32,4608]{1,0:T(8,128)}), f32[32,4608]{1,0:T(8,128)}) %all-reduce.5.cloned.1.call-update) | async-done | bytes 589840 | tf_op jit(solution)/shard_map/psum | solution.py:127
  355.5 1.3 fusion.97
  356.8 1.2 fusion.100
  358.0 50.4 %while.27 = (s32[]{:T(128)}, bf16[32,4608]{1,0:T(8,128)(2,1)S(1)}, bf16[8,32,4608]{2,1,0:T(8,128)(2,1)}, bf16[8,8,4608]{2,1,0:T(8,128)(2,1)}, bf16[8,4608]{1,0:T...) while((s32[]{:T(128)}, bf16[32,4608]{1,0:T(8,128)(2,1)S(1)}, ...), condition=%wide.region_13.14_spmd, body=%wide.region_10.13_spmd.sunk | while | flops 10036515 | bytes 3535725 | solution.py:133
  361.4 1.7 fusion.139
  367.7 1.7 fusion.139
  372.7 1.2 fusion.138
  374.0 1.7 fusion.139
  380.3 1.7 fusion.139
  386.6 1.7 fusion.139
  392.9 1.7 fusion.139
  399.1 1.7 fusion.139
  405.4 1.7 fusion.139
  408.4 4.6 %fusion.91 = bf16[256,4608]{1,0:T(8,128)(2,1)} fusion(f32[256,4608]{1,0:T(8,128)} %fusion.102, bf16[32,4608]{1,0:T(8,128)(2,1)S(1)} %get-tuple-element.159, s32[32]{0:T(128)S(1)} %sub.70), kind=kOutput, calls=%fused_computation.92 | convolution fusion | flops 79044608 | bytes 7372928 | tf_op jit(solution)/shard_map/dot_general | solution.py:138
  (120 shorter events, 55.0 us)
Async XLA Ops:
  7.2 23.5 %copy-start = (bf16[256,4608]{1,0:T(8,128)(2,1)S(1)}, bf16[256,4608]{1,0:T(8,128)(2,1)}, u32[]{:S(2)}) copy-start(bf16[256,4608]{1,0:T(8,128)(2,1)} %param.13) | copy-start | bytes 7077892
  7.2 24.9 %copy-start.4 = (bf16[4608]{0:T(1024)(128)(2,1)S(1)}, bf16[4608]{0:T(1024)(128)(2,1)}, u32[]{:S(2)}) copy-start(bf16[4608]{0:T(1024)(128)(2,1)} %param.17) | copy-start | bytes 27652
  7.2 24.9 %copy-start.3 = (bf16[2,1,4608]{2,0,1:T(2,128)(2,1)S(1)}, bf16[2,1,4608]{2,0,1:T(2,128)(2,1)}, u32[]{:S(2)}) copy-start(bf16[2,1,4608]{2,0,1:T(2,128)(2,1)} %param.14) | copy-start | bytes 55300
  7.2 30.8 %copy-start.1 = (bf16[2,1,8,4608]{3,2,1,0:T(8,128)(2,1)S(1)}, bf16[2,1,8,4608]{3,2,1,0:T(8,128)(2,1)}, u32[]{:S(2)}) copy-start(bf16[2,1,8,4608]{3,2,1,0:T(8,128)(2,1)} %param.15) | copy-start | bytes 442372
  7.2 39.0 %copy-start.2 = (bf16[2,1,8,4608]{3,2,1,0:T(8,128)(2,1)S(1)}, bf16[2,1,8,4608]{3,2,1,0:T(8,128)(2,1)}, u32[]{:S(2)}) copy-start(bf16[2,1,8,4608]{3,2,1,0:T(8,128)(2,1)} %param.16) | copy-start | bytes 442372
  7.2 147.8 %all-reduce.3.cloned.1.call-start = ((), (), s32[]{:S(2)}) async-start(), calls=%async_computation | async-start | bytes 589824 | tf_op jit(solution)/shard_map/psum | solution.py:94
  31.9 323.5 %all-reduce.5.cloned.1.call-start = ((), (), s32[]{:S(2)}) async-start(), calls=%async_computation.1 | async-start | bytes 1179648 | tf_op jit(solution)/shard_map/psum | solution.py:127
Sparse Core Ops, SparseCore 0:
  32.0 122.9 all-reduce.2
  228.3 127.1 all-reduce.4
where the time goes:
time: 422 us; the launch traced here: 420 us
  waiting for transfers between devices  224 us (53%)
  blocking collectives  85 us (20%)
  matrix products  47.9 us (11%)
  other arithmetic  40 us (9%)
  between operations  14.1 us (3%)
  local copies, waits for them, and re-layouts  7.85 us (2%)
    psum x1, waiting for transfers between devices, per_device(): head_in_grad = lax.psum(partial_value, ('section', 'dp'))  124 us
    psum x1, waiting for transfers between devices, per_device(): looked = lax.psum(looked, ('section', 'dp')).astype(jnp.float32)  101 us
    psum x1, blocking collectives, per_device(): lax.psum(jnp.stack([jnp.sum(powers, axis=1), jnp.sum(jnp.where(target_mas...  41.2 us
    all_gather x1, blocking collectives, per_device(): lax.all_gather(jnp.concatenate([token_ids, target_ids], 0), 'dp', axis=1,...  22.3 us
    dot_general x8, matrix products, layer_backward(): jnp.dot(preact_grad, first_proj, preferred_element_type=jnp.float32)  14 us
    dot_general x8, matrix products, layer_forward(): branch = jnp.dot(hidden, second_proj, preferred_element_type=jnp.float32)  12.8 us
    reduce_sum x17, other arithmetic, normalize(): scale = lax.rsqrt(jnp.mean(values * values, axis=-1, keepdims=True) + EPS)  10.7 us
    dot_general x8, matrix products, layer_backward(): lax.dot_general(activated, first_proj, (((1,), (1,)), ((), ())), preferre...  9.88 us
  transfers between devices with their start and end apart: 2, of which 2 were waited for; matrix products, arithmetic and copies ran while one was open for 1% of the time, Pallas kernels for 0%

commit v1 on v0

--- a/solution.py
+++ b/solution.py
@@ -7,6 +7,7 @@
 EPS = 1e-06
 CAP = 30.0
 GELU_C = 0.7978845608028654
+order_frames = lambda point: lax.psum(lax.psum(point, "dp"), axis_name="section")
 
 
 def shifted(block, axis, distance):
@@ -91,7 +92,7 @@
         jnp.bfloat16
     )
     looked = jnp.dot(chosen, table, preferred_element_type=jnp.float32).astype(jnp.bfloat16)
-    looked = lax.psum(looked, ("section", "dp")).astype(jnp.float32)
+    looked = order_frames(looked).astype(jnp.float32)
     rows = (looked * embed_scale).astype(jnp.bfloat16)
 
     def forward(rows, weights):

time: 422 us -> 400 us (0.948)
  waiting for transfers between devices: 224 us -> 204 us
    psum x1 -> x2, waiting for transfers between devices: 101 us -> 79.7 us  [the longest x1 54.1 us: lax.psum(point, 'dp')]
  transfers between devices with their start and end apart: 2 -> 3, of which waited for: 2 -> 3; matrix products, arithmetic and copies ran while one was open for 1% -> 1% of each run, Pallas kernels for 0% -> 0%
where the time goes in v1:
time: 400 us; the launch traced here: 397 us
  waiting for transfers between devices  204 us (51%)
  blocking collectives  82.9 us (21%)
  matrix products  47.9 us (12%)
  other arithmetic  40 us (10%)
  between operations  13.9 us (3%)
  local copies, waits for them, and re-layouts  7.85 us (2%)
    psum x1, waiting for transfers between devices, per_device(): head_in_grad = lax.psum(partial_value, ('section', 'dp'))  125 us
    psum x1, waiting for transfers between devices, lax.psum(point, 'dp')  54.1 us
    psum x1, blocking collectives, per_device(): lax.psum(jnp.stack([jnp.sum(powers, axis=1), jnp.sum(jnp.where(target_mas...  39.4 us
    psum x1, waiting for transfers between devices, lax.psum(lax.psum(point, 'dp'), axis_name='section')  25.7 us
    all_gather x1, blocking collectives, per_device(): lax.all_gather(jnp.concatenate([token_ids, target_ids], 0), 'dp', axis=1,...  22.3 us
    dot_general x8, matrix products, layer_backward(): jnp.dot(preact_grad, first_proj, preferred_element_type=jnp.float32)  14 us
    dot_general x8, matrix products, layer_forward(): branch = jnp.dot(hidden, second_proj, preferred_element_type=jnp.float32)  12.8 us
    reduce_sum x17, other arithmetic, normalize(): scale = lax.rsqrt(jnp.mean(values * values, axis=-1, keepdims=True) + EPS)  10.7 us
  transfers between devices with their start and end apart: 3, of which 3 were waited for; matrix products, arithmetic and copies ran while one was open for 1% of the time, Pallas kernels for 0%

profile of v1, /device:TPU:0, one launch (start us, length us, event | category | flops | bytes accessed | tf_op | source)
XLA Modules:
  0.0 397.4 jit_solution(5556878007330996495)
XLA Ops:
  8.2 22.3 %all-gather = s32[8,2,4]{2,1,0:T(2,128)S(1)} all-gather(s32[1,2,4]{2,1,0:T(2,128)S(1)} %bitcast.102), channel_id=1, replica_groups=mesh['section'=4,'dp'=8] {'dp'}, dimensions={0}, use_global_device_ids=true | all-gather | bytes 288 | tf_op jit(solution)/shard_map/all_gather | solution.py:84
  30.6 1.2 convolution_convert_fusion
  32.1 5.3 %all_gather.13 = bf16[2,4,4608]{2,0,1:T(2,128)(2,1)S(1)} all-gather(bf16[2,1,4608]{2,0,1:T(2,128)(2,1)S(1)} %copy-done.3), channel_id=1, replica_groups=mesh['section'=4,'dp'=8] {'section'}, dimensions={1}, use_global_device_ids=true | all-gather | bytes 92160 | tf_op jit(solution)/shard_map/all_gather | solution.py:85
  38.0 8.1 %all_gather.14 = bf16[2,4,8,4608]{3,2,1,0:T(8,128)(2,1)} all-gather(bf16[2,1,8,4608]{3,2,1,0:T(8,128)(2,1)S(1)} %copy-done.1), channel_id=1, replica_groups=mesh['section'=4,'dp'=8] {'section'}, dimensions={1}, use_global_device_ids=true | all-gather | bytes 737280 | tf_op jit(solution)/shard_map/all_gather | solution.py:86
  46.1 54.1 %all-reduce.4.cloned.1.call-done = bf16[32,4608]{1,0:T(8,128)(2,1)} async-done(((bf16[32,4608]{1,0:T(8,128)(2,1)}), bf16[32,4608]{1,0:T(8,128)(2,1)}) %all-reduce.4.cloned.1.call-update) | async-done | bytes 294928 | tf_op jit(solution)/shard_map/psum | solution.py:10
  100.2 8.0 %all_gather.15 = bf16[2,4,8,4608]{3,2,1,0:T(8,128)(2,1)} all-gather(bf16[2,1,8,4608]{3,2,1,0:T(8,128)(2,1)S(1)} %copy-done.2), channel_id=1, replica_groups=mesh['section'=4,'dp'=8] {'section'}, dimensions={1}, use_global_device_ids=true | all-gather | bytes 737280 | tf_op jit(solution)/shard_map/all_gather | solution.py:87
  108.2 25.7 %all-reduce.6.cloned.1.call-done = bf16[32,4608]{1,0:T(8,128)(2,1)} async-done(((bf16[32,4608]{1,0:T(8,128)(2,1)}), bf16[32,4608]{1,0:T(8,128)(2,1)}) %all-reduce.6.cloned.1.call-update) | async-done | bytes 294928 | tf_op jit(solution)/shard_map/psum | solution.py:10
  134.9 28.2 %while.26 = (s32[]{:T(128)}, bf16[32,4608]{1,0:T(8,128)(2,1)S(1)}, bf16[8,32,4608]{2,1,0:T(8,128)(2,1)}, bf16[8,4608]{1,0:T(8,128)(2,1)}, bf16[8,8,4608]{2,1,0:T...) while((s32[]{:T(128)}, bf16[32,4608]{1,0:T(8,128)(2,1)S(1)}, bf16[8,32,4608]{2,1,0:T(8,128)(2,1)}, ...), condition=%wide.region_4.5_spmd, body=%wide.region_2.4_spmd.sunk | while | flops 6200098 | bytes 2556893 | solution.py:101
  136.8 1.6 fusion.132
  140.4 1.6 fusion.132
  143.9 1.6 fusion.132
  147.4 1.6 fusion.132
  151.0 1.6 fusion.132
  154.5 1.6 fusion.132
  158.0 1.6 fusion.132
  161.6 1.6 fusion.132
  164.3 39.4 %psum.30 = f32[2,32]{1,0:T(2,128)S(1)} all-reduce(f32[2,32]{1,0:T(2,128)S(1)} %pad_maximum_fusion), channel_id=1, replica_groups=mesh['section'=4,'dp'=8] {'section','dp'}, use_global_device_ids=true, to_apply=%region_8.9 | all-reduce | flops 64 | bytes 512 | tf_op jit(solution)/shard_map/psum | solution.py:112
  203.8 1.4 fusion.107
  205.8 3.0 fusion.102
  208.8 124.5 %all-reduce.8.cloned.1.call-done = f32[32,4608]{1,0:T(8,128)} async-done(((f32[32,4608]{1,0:T(8,128)}), f32[32,4608]{1,0:T(8,128)}) %all-reduce.8.cloned.1.call-update) | async-done | bytes 589840 | tf_op jit(solution)/shard_map/psum | solution.py:128
  333.4 1.3 fusion.97
  334.7 1.2 fusion.100
  335.9 50.3 %while.27 = (s32[]{:T(128)}, bf16[32,4608]{1,0:T(8,128)(2,1)S(1)}, bf16[8,32,4608]{2,1,0:T(8,128)(2,1)}, bf16[8,8,4608]{2,1,0:T(8,128)(2,1)}, bf16[8,4608]{1,0:T...) while((s32[]{:T(128)}, bf16[32,4608]{1,0:T(8,128)(2,1)S(1)}, ...), condition=%wide.region_14.15_spmd, body=%wide.region_11.14_spmd.sunk | while | flops 10036515 | bytes 3535725 | solution.py:134
  339.3 1.7 fusion.139
  345.6 1.7 fusion.139
  351.9 1.7 fusion.139
  358.2 1.7 fusion.139
  364.5 1.7 fusion.139
  370.7 1.7 fusion.139
  377.0 1.7 fusion.139
  383.3 1.7 fusion.139
  386.3 4.6 %fusion.91 = bf16[256,4608]{1,0:T(8,128)(2,1)} fusion(f32[256,4608]{1,0:T(8,128)} %fusion.102, bf16[32,4608]{1,0:T(8,128)(2,1)S(1)} %get-tuple-element.159, s32[32]{0:T(128)S(1)} %sub.70), kind=kOutput, calls=%fused_computation.92 | convolution fusion | flops 79044608 | bytes 7372928 | tf_op jit(solution)/shard_map/dot_general | solution.py:139
  (123 shorter events, 56.3 us)
Async XLA Ops:
  7.2 23.5 %copy-start = (bf16[256,4608]{1,0:T(8,128)(2,1)S(1)}, bf16[256,4608]{1,0:T(8,128)(2,1)}, u32[]{:S(2)}) copy-start(bf16[256,4608]{1,0:T(8,128)(2,1)} %param.13) | copy-start | bytes 7077892
  7.2 24.9 %copy-start.4 = (bf16[4608]{0:T(1024)(128)(2,1)S(1)}, bf16[4608]{0:T(1024)(128)(2,1)}, u32[]{:S(2)}) copy-start(bf16[4608]{0:T(1024)(128)(2,1)} %param.17) | copy-start | bytes 27652
  7.2 24.9 %copy-start.3 = (bf16[2,1,4608]{2,0,1:T(2,128)(2,1)S(1)}, bf16[2,1,4608]{2,0,1:T(2,128)(2,1)}, u32[]{:S(2)}) copy-start(bf16[2,1,4608]{2,0,1:T(2,128)(2,1)} %param.14) | copy-start | bytes 55300
  7.2 30.8 %copy-start.1 = (bf16[2,1,8,4608]{3,2,1,0:T(8,128)(2,1)S(1)}, bf16[2,1,8,4608]{3,2,1,0:T(8,128)(2,1)}, u32[]{:S(2)}) copy-start(bf16[2,1,8,4608]{3,2,1,0:T(8,128)(2,1)} %param.15) | copy-start | bytes 442372
  7.2 93.0 %copy-start.2 = (bf16[2,1,8,4608]{3,2,1,0:T(8,128)(2,1)S(1)}, bf16[2,1,8,4608]{3,2,1,0:T(8,128)(2,1)}, u32[]{:S(2)}) copy-start(bf16[2,1,8,4608]{3,2,1,0:T(8,128)(2,1)} %param.16) | copy-start | bytes 442372
  7.2 92.9 %all-reduce.4.cloned.1.call-start = ((), (), s32[]{:S(2)}) async-start(), calls=%async_computation | async-start | bytes 589824 | tf_op jit(solution)/shard_map/psum | solution.py:10
  31.9 102.0 %all-reduce.6.cloned.1.call-start = ((), (), s32[]{:S(2)}) async-start(), calls=%async_computation.1 | async-start | bytes 589824 | tf_op jit(solution)/shard_map/psum | solution.py:10
  100.2 233.2 %all-reduce.8.cloned.1.call-start = ((), (), s32[]{:S(2)}) async-start(), calls=%async_computation.2 | async-start | bytes 1179648 | tf_op jit(solution)/shard_map/psum | solution.py:128
Sparse Core Ops, SparseCore 0:
  32.0 68.0 all-reduce.3
  102.6 31.2 all-reduce.5
  205.3 127.9 all-reduce.7
